TPU v7x, 32 devices: a whole 2x2x4 slice. The times are simulated.
32 devices in a mesh: row: 16 (over z, x, core), col: 2 (over y).
Axes of the slice: x: 2, y: 2, z: 4, core: 2. Of those that a mesh axis runs over, the one named last changes fastest.
Arguments:
- counts: int32 [8192, 32768], P('row', 'col'), may hold values from 0 to 63
- row_support: int32 [8192], P(('row', 'col')), may hold values from 1 to 2209
- col_support: int32 [32768], P(('col', 'row')), may hold values from 1 to 2209
- total: int32 [1], replicated, may hold values from 256 to 4095
- sketch: bfloat16 [32768, 256], P('col'), may hold values from -6 to 6
Outputs:
- left_basis: float32 [8192, 256], P('row')
- right_basis: float32 [32768, 256], P('col')
All inputs are finite; a program needn't handle non-finite values.
Results may differ from a plain program's by a relative error of at most 0.012.
Values may be sent and summed in bfloat16 or wider, within the bound.
A program may use at most 192 MiB of HBM per device.

v0:
```python
import jax
import jax.numpy as jnp
from jax import lax
from jax.sharding import PartitionSpec as P


def lift(block, row_part, col_part, total):
    value = jnp.log(jnp.maximum(block, 1).astype(jnp.float32))
    value = value + jnp.log(total[0].astype(jnp.float32))
    value = value - jnp.log(row_part.astype(jnp.float32))[:, None]
    value = value - jnp.log(col_part.astype(jnp.float32))[None, :]
    return jnp.where(block > 0, jnp.maximum(value, 0.0), 0.0).astype(jnp.bfloat16)


def factor_of(gram):
    return jnp.linalg.cholesky(gram)


def solve_rows(lower, matrix):
    return jax.scipy.linalg.solve_triangular(lower, matrix.T, lower=True).T


def gram_of(matrix):
    return jnp.dot(matrix.T, matrix, precision=lax.Precision.HIGHEST)


def per_device(counts, row_support, col_support, total, sketch):
    row_local = lax.all_gather(row_support, "col", axis=0, tiled=True)
    col_local = lax.all_gather(col_support, "row", axis=0, tiled=True)
    table = lift(counts, row_local, col_local, total)
    row_count = table.shape[0]
    col_count = table.shape[1]

    def left_orth(rhs, narrow):
        whole = lax.psum(jnp.dot(table, rhs, preferred_element_type=jnp.float32), "col")
        gram = lax.psum(gram_of(whole), "row")
        basis = solve_rows(factor_of(gram), whole)
        if narrow:
            return basis.astype(jnp.bfloat16)
        return basis

    q_first = left_orth(sketch, True)
    partial_value = lax.dot_general(
        table, q_first, (((0,), (0,)), ((), ())), preferred_element_type=jnp.float32
    )
    whole = lax.psum(partial_value, "row")
    gram = lax.psum(gram_of(whole), "col")
    q_second = solve_rows(factor_of(gram), whole)
    q_third = left_orth(q_second.astype(jnp.bfloat16), False)
    total_rows = row_count * lax.axis_size("row")
    total_cols = col_count * lax.axis_size("col")
    return (
        q_third * jnp.sqrt(jnp.float32(total_rows)),
        q_second * jnp.sqrt(jnp.float32(total_cols)),
    )


def solution(mesh):
    in_specs = (P("row", "col"), P(("row", "col")), P(("col", "row")), P(), P("col", None))
    out_specs = (P("row", None), P("col", None))
    return jax.shard_map(
        per_device, mesh=mesh, in_specs=in_specs, out_specs=out_specs, check_vma=False
    )
```

profile of v0, /device:TPU:0, one launch (start us, length us, event | category | flops | bytes accessed | tf_op | source)
XLA Modules:
  0.0 932.7 jit_solution(9221446948077840741)
XLA Ops:
  7.2 23.5 %all_gather.7 = s32[16384]{0:T(1024)S(1)} all-gather(s32[1024]{0:T(1024)} %param.10), channel_id=1, replica_groups=mesh['row'=16,'col'=2] {'row'}, dimensions={0}, use_global_device_ids=true | all-gather | bytes 69632 | tf_op jit(solution)/shard_map/all_gather | solution.py:29
  30.7 4.5 all-gather
  35.9 17.1 %select_convert_fusion = bf16[512,16384]{1,0:T(8,128)(2,1)S(1)} fusion(s32[512,16384]{1,0:T(8,128)} %param.8, f32[16384]{0:T(1024)S(1)} %convert_log_fusion, f32[512]{0:T(512)S(1)} %bitcast.119, f32[]{:T(128)} %bitcast), kind=kLoop, calls=%fused_computation.6 | loop fusion | flops 75497472 | bytes 50399236 | tf_op jit(solution)/shard_map/convert_element_type | solution.py:12
  53.0 6.2 copy-done.2
  59.2 7.7 fusion.42
  67.0 26.0 %all-reduce.8.cloned.1.call-done = f32[512,256]{1,0:T(8,128)} async-done(((f32[512,256]{1,0:T(8,128)}), f32[512,256]{1,0:T(8,128)}) %all-reduce.8.cloned.1.call-update) | async-done | bytes 524304 | tf_op jit(solution)/shard_map/psum | solution.py:35
  93.0 2.9 fusion.43
  96.2 90.5 %all-reduce.10.cloned.1.call-done = f32[256,256]{0,1:T(8,128)} async-done(((f32[256,256]{0,1:T(8,128)}), f32[256,256]{0,1:T(8,128)}) %all-reduce.10.cloned.1.call-update) | async-done | bytes 262160 | tf_op jit(solution)/shard_map/psum | solution.py:36
  186.8 1.1 copy.16
  188.8 11.7 %cholesky.172 = f32[128,128]{1,0:T(8,128)S(1)} custom-call(f32[128,128]{1,0:T(8,128)S(1)} %cholesky.270), custom_call_target="Cholesky" | custom-call | tf_op jit(solution)/shard_map/jit(cholesky)/cholesky | solution.py:16
  200.6 9.8 %custom-call.19 = f32[1,128,128]{1,2,0:T(8,128)S(1)} custom-call(f32[1,128,128]{2,1,0:T(8,128)S(1)} %get-tuple-element.73), custom_call_target="InvertDiagBlocksLowerTriangular" | custom-call | tf_op jit(solution)/shard_map/jit(cholesky)/cholesky | solution.py:16
  210.9 11.7 %cholesky.189 = f32[128,128]{1,0:T(8,128)S(1)} custom-call(f32[128,128]{1,0:T(8,128)S(1)} %convolution_subtract_fusion.5), custom_call_target="Cholesky" | custom-call | tf_op jit(solution)/shard_map/jit(cholesky)/cholesky | solution.py:16
  224.9 4.5 while.6
  225.9 1.4 bitcast_dynamic-update-slice_fusion.7
  227.9 1.4 bitcast_dynamic-update-slice_fusion.7
  229.4 19.7 %custom-call.20 = f32[2,128,128]{1,2,0:T(8,128)S(1)} custom-call(f32[2,128,128]{2,1,0:T(8,128)S(1)} %get-tuple-element.26), custom_call_target="InvertDiagBlocksLowerTriangular" | custom-call | tf_op jit(solution)/shard_map/jit(_solve_triangular)/triangular_solve | solution.py:20
  249.1 1.4 fusion.9
  250.4 1.5 convolution_subtract_fusion.2
  252.4 16.1 %fusion.6 = f32[16384,256]{1,0:T(8,128)} fusion(bf16[512,16384]{1,0:T(8,128)(2,1)} %copy-done.2, bf16[128,512]{1,0:T(8,128)(2,1)S(1)} %fusion.23, f32[128,512]{1,0:T(8,128)S(1)} %fusion.9), kind=kOutput, calls=%fused_computation.25 | convolution fusion | flops 4295491584 | bytes 33947648 | tf_op jit(solution)/shard_map/dot_general | solution.py:43
  268.6 298.5 %all-reduce.12.cloned.1.call-done = f32[16384,256]{1,0:T(8,128)} async-done(((f32[16384,256]{1,0:T(8,128)}), f32[16384,256]{1,0:T(8,128)}) %all-reduce.12.cloned.1.call-update) | async-done | bytes 16777232 | tf_op jit(solution)/shard_map/psum | solution.py:46
  567.1 37.8 %fusion.44 = f32[256,256]{0,1:T(8,128)} fusion(f32[16384,256]{1,0:T(8,128)} %all-reduce.12.cloned.1.call-done), kind=kOutput, calls=%fused_computation.95 | convolution fusion | flops 12884901888 | bytes 17039360 | tf_op jit(solution)/shard_map/dot_general | solution.py:24
  605.0 23.0 %all-reduce.14.cloned.1.call-done = f32[256,256]{0,1:T(8,128)} async-done(((f32[256,256]{0,1:T(8,128)}), f32[256,256]{0,1:T(8,128)}) %all-reduce.14.cloned.1.call-update) | async-done | bytes 262160 | tf_op jit(solution)/shard_map/psum | solution.py:47
  628.0 1.1 copy.18
  630.1 11.7 %cholesky.206 = f32[128,128]{1,0:T(8,128)S(1)} custom-call(f32[128,128]{1,0:T(8,128)S(1)} %cholesky.273), custom_call_target="Cholesky" | custom-call | tf_op jit(solution)/shard_map/jit(cholesky)/cholesky | solution.py:16
  641.9 9.8 %custom-call.21 = f32[1,128,128]{1,2,0:T(8,128)S(1)} custom-call(f32[1,128,128]{2,1,0:T(8,128)S(1)} %get-tuple-element.69), custom_call_target="InvertDiagBlocksLowerTriangular" | custom-call | tf_op jit(solution)/shard_map/jit(cholesky)/cholesky | solution.py:16
  652.2 11.7 %cholesky.223 = f32[128,128]{1,0:T(8,128)S(1)} custom-call(f32[128,128]{1,0:T(8,128)S(1)} %convolution_subtract_fusion.4), custom_call_target="Cholesky" | custom-call | tf_op jit(solution)/shard_map/jit(cholesky)/cholesky | solution.py:16
  666.5 3.8 while.5
  667.1 1.3 bitcast_dynamic-update-slice_fusion.6
  669.0 1.3 bitcast_dynamic-update-slice_fusion.6
  670.3 19.7 %custom-call.15 = f32[2,128,128]{1,2,0:T(8,128)S(1)} custom-call(f32[2,128,128]{2,1,0:T(8,128)S(1)} %get-tuple-element.19), custom_call_target="InvertDiagBlocksLowerTriangular" | custom-call | tf_op jit(solution)/shard_map/jit(_solve_triangular)/triangular_solve | solution.py:20
  690.0 10.8 %fusion.3 = f32[128,16384]{1,0:T(8,128)S(1)} fusion(f32[256,16384]{0,1:T(8,128)} %bitcast.113, f32[2,128,128]{1,2,0:T(8,128)S(1)} %custom-call.15), kind=kOutput, calls=%fused_computation.12 | convolution fusion | flops 3221225472 | bytes 16842752 | tf_op jit(solution)/shard_map/jit(_solve_triangular)/triangular_solve | solution.py:20
  700.8 13.4 %convolution_subtract_fusion = f32[128,16384]{0,1:T(8,128)S(1)} fusion(f32[128,16384]{1,0:T(8,128)S(1)} %fusion.3, f32[256,16384]{0,1:T(8,128)S(1)} %bitcast.114, f32[256,256]{1,0:T(8,128)S(1)} %get-tuple-element.225), kind=kOutput, calls=%fused_computation.7 | convolution fusion | flops 3223322624 | bytes 25231360 | tf_op jit(solution)/shard_map/jit(_solve_triangular)/triangular_solve | solution.py:20
  714.2 9.8 %fusion.19 = f32[128,16384]{1,0:T(8,128)} fusion(f32[128,16384]{0,1:T(8,128)S(1)} %convolution_subtract_fusion, f32[2,128,128]{1,2,0:T(8,128)S(1)} %custom-call.15), kind=kOutput, calls=%fused_computation.45 | convolution fusion | flops 3221225472 | bytes 16842752 | tf_op jit(solution)/shard_map/jit(_solve_triangular)/triangular_solve | solution.py:20
  724.0 13.7 %fusion.1 = f32[512,256]{1,0:T(8,128)} fusion(bf16[512,16384]{1,0:T(8,128)(2,1)} %copy-done.2, f32[128,16384]{1,0:T(8,128)} %fusion.19, f32[128,16384]{1,0:T(8,128)} %copy-done.1), kind=kOutput, calls=%fused_computation.11 | convolution fusion | flops 4311744512 | bytes 34078720 | tf_op jit(solution)/shard_map/dot_general | solution.py:35
  737.8 28.8 %all-reduce.16.cloned.1.call-done = f32[512,256]{1,0:T(8,128)} async-done(((f32[512,256]{1,0:T(8,128)}), f32[512,256]{1,0:T(8,128)}) %all-reduce.16.cloned.1.call-update) | async-done | bytes 524304 | tf_op jit(solution)/shard_map/psum | solution.py:35
  766.6 2.9 fusion.45
  769.5 12.1 %multiply_bitcast_fusion = f32[16384,256]{0,1:T(8,128)} fusion(f32[128,16384]{1,0:T(8,128)} %fusion.19, f32[128,16384]{1,0:T(8,128)} %copy-done.1), kind=kLoop, calls=%fused_computation.9 | loop fusion | flops 8388608 | bytes 33554432 | tf_op jit(solution)/shard_map/mul | solution.py:54
  781.6 17.5 %copy.22 = f32[16384,256]{1,0:T(8,128)} copy(f32[16384,256]{0,1:T(8,128)} %multiply_bitcast_fusion) | data formatting | bytes 33554432
  799.2 61.0 %all-reduce.18.cloned.1.call-done = f32[256,256]{0,1:T(8,128)} async-done(((f32[256,256]{0,1:T(8,128)}), f32[256,256]{0,1:T(8,128)}) %all-reduce.18.cloned.1.call-update) | async-done | bytes 262160 | tf_op jit(solution)/shard_map/psum | solution.py:36
  860.1 1.1 copy.20
  862.2 11.7 %cholesky.240 = f32[128,128]{1,0:T(8,128)S(1)} custom-call(f32[128,128]{1,0:T(8,128)S(1)} %cholesky.276), custom_call_target="Cholesky" | custom-call | tf_op jit(solution)/shard_map/jit(cholesky)/cholesky | solution.py:16
  874.0 9.8 %custom-call.22 = f32[1,128,128]{1,2,0:T(8,128)S(1)} custom-call(f32[1,128,128]{2,1,0:T(8,128)S(1)} %get-tuple-element.65), custom_call_target="InvertDiagBlocksLowerTriangular" | custom-call | tf_op jit(solution)/shard_map/jit(cholesky)/cholesky | solution.py:16
  884.3 11.7 %cholesky.257 = f32[128,128]{1,0:T(8,128)S(1)} custom-call(f32[128,128]{1,0:T(8,128)S(1)} %convolution_subtract_fusion.3), custom_call_target="Cholesky" | custom-call | tf_op jit(solution)/shard_map/jit(cholesky)/cholesky | solution.py:16
  898.8 4.1 while.7
  899.4 1.4 bitcast_dynamic-update-slice_fusion.8
  901.5 1.4 bitcast_dynamic-update-slice_fusion.8
  902.9 20.0 %custom-call.23 = f32[2,128,128]{1,2,0:T(8,128)S(1)} custom-call(f32[2,128,128]{2,1,0:T(8,128)S(1)} %get-tuple-element.27), custom_call_target="InvertDiagBlocksLowerTriangular" | custom-call | tf_op jit(solution)/shard_map/jit(_solve_triangular)/triangular_solve | solution.py:20
  924.4 1.0 copy.21
  (72 shorter events, 14.3 us)
Async XLA Ops:
  7.2 85.9 %all-reduce.8.cloned.1.call-start = ((), (), s32[]{:S(2)}) async-start(), calls=%async_computation | async-start | bytes 1048576 | tf_op jit(solution)/shard_map/psum | solution.py:35
  53.0 6.2 copy-start.2
  67.0 119.8 %all-reduce.10.cloned.1.call-start = ((), (), s32[]{:S(2)}) async-start(), calls=%async_computation.1 | async-start | bytes 524288 | tf_op jit(solution)/shard_map/psum | solution.py:36
  96.0 471.1 %all-reduce.12.cloned.1.call-start = ((), (), s32[]{:S(2)}) async-start(), calls=%async_computation.2 | async-start | bytes 33554432 | tf_op jit(solution)/shard_map/psum | solution.py:46
  268.5 359.5 %all-reduce.14.cloned.1.call-start = ((), (), s32[]{:S(2)}) async-start(), calls=%async_computation.3 | async-start | bytes 524288 | tf_op jit(solution)/shard_map/psum | solution.py:47
  605.0 161.6 %all-reduce.16.cloned.1.call-start = ((), (), s32[]{:S(2)}) async-start(), calls=%async_computation.4 | async-start | bytes 1048576 | tf_op jit(solution)/shard_map/psum | solution.py:35
  690.0 10.8 %copy-start = (f32[16384,256]{1,0:T(8,128)S(1)}, f32[16384,256]{1,0:T(8,128)}, u32[]{:S(2)}) copy-start(f32[16384,256]{1,0:T(8,128)} %all-reduce.12.cloned.1.call-done) | copy-start | bytes 50331652
  700.8 13.4 %copy-start.1 = (f32[128,16384]{1,0:T(8,128)}, f32[128,16384]{1,0:T(8,128)S(1)}, u32[]{:S(2)}) copy-start(f32[128,16384]{1,0:T(8,128)S(1)} %fusion.3) | copy-start | bytes 25165828
  737.7 122.4 %all-reduce.18.cloned.1.call-start = ((), (), s32[]{:S(2)}) async-start(), calls=%async_computation.5 | async-start | bytes 524288 | tf_op jit(solution)/shard_map/psum | solution.py:36
  781.6 141.2 %copy-start.3 = (f32[512,256]{1,0:T(8,128)S(1)}, f32[512,256]{1,0:T(8,128)}, u32[]{:S(2)}) copy-start(f32[512,256]{1,0:T(8,128)} %all-reduce.16.cloned.1.call-done) | copy-start | bytes 1572868
Sparse Core Ops, SparseCore 0:
  67.1 25.9 all-reduce.7
  97.0 89.7 all-reduce.9
  268.7 298.4 all-reduce.11
  605.1 22.9 all-reduce.13
  737.9 28.6 all-reduce.15
  770.4 89.6 all-reduce.17
where the time goes:
time: 938 us; the launch traced here: 933 us
  waiting for transfers between devices  528 us (56%)
  other arithmetic  195 us (21%)
  matrix products  121 us (13%)
  local copies, waits for them, and re-layouts  40 us (4%)
  blocking collectives  28 us (3%)
  between operations  19.6 us (2%)
    psum x1, waiting for transfers between devices, per_device(): whole = lax.psum(partial_value, 'row')  299 us
    psum x2, waiting for transfers between devices, left_orth(): gram = lax.psum(gram_of(whole), 'row')  151 us
    another operation x20, other arithmetic, factor_of(): return jnp.linalg.cholesky(gram)  103 us
    another operation x7, other arithmetic, solve_rows(): return jax.scipy.linalg.solve_triangular(lower, matrix.T, lower=True).T  59.4 us
    psum x2, waiting for transfers between devices, left_orth(): lax.psum(jnp.dot(table, rhs, preferred_element_type=jnp.float32), 'col')  54.8 us
    dot_general x3, matrix products, gram_of(): return jnp.dot(matrix.T, matrix, precision=lax.Precision.HIGHEST)  43.6 us
    another operation x9, matrix products, solve_rows(): return jax.scipy.linalg.solve_triangular(lower, matrix.T, lower=True).T  38.7 us
    unnamed x10, local copies, waits for them, and re-layouts  24.7 us
  transfers between devices with their start and end apart: 6, of which 6 were waited for; matrix products, arithmetic and copies ran while one was open for 3% of the time, Pallas kernels for 0%

commit v1 on v0

--- a/solution.py
+++ b/solution.py
@@ -33,7 +33,8 @@
 
     def left_orth(rhs, narrow):
         whole = lax.psum(jnp.dot(table, rhs, preferred_element_type=jnp.float32), "col")
-        gram = lax.psum(gram_of(whole), "row")
+        check_rounds = lambda u, dev_axis: jax.lax.all_gather(u, dev_axis).sum(axis=0)
+        gram = check_rounds(gram_of(whole), "row")
         basis = solve_rows(factor_of(gram), whole)
         if narrow:
             return basis.astype(jnp.bfloat16)

time: 938 us -> 857 us (0.914)
  waiting for transfers between devices: 528 us -> 445 us
    psum x2 -> x0, waiting for transfers between devices: 151 us -> none  [left_orth(): gram = lax.psum(gram_of(whole), 'row')]
    all_gather x0 -> x2, waiting for transfers between devices: none -> 70.8 us  [left_orth(): jax.lax.all_gather(u, dev_axis).sum(axis=0)]
  transfers between devices with their start and end apart: 6 -> 6, of which waited for: 6 -> 6; matrix products, arithmetic and copies ran while one was open for 3% -> 4% of each run, Pallas kernels for 0% -> 0%
where the time goes in v1:
time: 857 us; the launch traced here: 851 us
  waiting for transfers between devices  445 us (52%)
  other arithmetic  198 us (23%)
  matrix products  121 us (14%)
  local copies, waits for them, and re-layouts  38.1 us (4%)
  blocking collectives  28 us (3%)
  between operations  19.3 us (2%)
    psum x1, waiting for transfers between devices, per_device(): whole = lax.psum(partial_value, 'row')  297 us
    another operation x20, other arithmetic, factor_of(): return jnp.linalg.cholesky(gram)  103 us
    all_gather x2, waiting for transfers between devices, left_orth(): jax.lax.all_gather(u, dev_axis).sum(axis=0)  70.8 us
    another operation x7, other arithmetic, solve_rows(): return jax.scipy.linalg.solve_triangular(lower, matrix.T, lower=True).T  59.3 us
    psum x2, waiting for transfers between devices, left_orth(): lax.psum(jnp.dot(table, rhs, preferred_element_type=jnp.float32), 'col')  54.8 us
    dot_general x3, matrix products, gram_of(): return jnp.dot(matrix.T, matrix, precision=lax.Precision.HIGHEST)  43.7 us
    another operation x9, matrix products, solve_rows(): return jax.scipy.linalg.solve_triangular(lower, matrix.T, lower=True).T  38.7 us
    unnamed x10, local copies, waits for them, and re-layouts  24.7 us
  transfers between devices with their start and end apart: 6, of which 6 were waited for; matrix products, arithmetic and copies ran while one was open for 4% of the time, Pallas kernels for 0%

profile of v1, /device:TPU:0, one launch (start us, length us, event | category | flops | bytes accessed | tf_op | source)
XLA Modules:
  0.0 851.4 jit_solution(6707301712329133888)
XLA Ops:
  7.2 23.5 %all_gather.19 = s32[16384]{0:T(1024)S(1)} all-gather(s32[1024]{0:T(1024)} %param.10), channel_id=1, replica_groups=mesh['row'=16,'col'=2] {'row'}, dimensions={0}, use_global_device_ids=true | all-gather | bytes 69632 | tf_op jit(solution)/shard_map/all_gather | solution.py:29
  30.7 4.5 all-gather.2
  35.9 17.1 %select_convert_fusion = bf16[512,16384]{1,0:T(8,128)(2,1)S(1)} fusion(s32[512,16384]{1,0:T(8,128)} %param.8, f32[16384]{0:T(1024)S(1)} %convert_log_fusion, f32[512]{0:T(512)S(1)} %bitcast.123, f32[]{:T(128)} %bitcast), kind=kLoop, calls=%fused_computation.6 | loop fusion | flops 75497472 | bytes 50399236 | tf_op jit(solution)/shard_map/convert_element_type | solution.py:12
  53.0 6.2 copy-done.2
  59.2 7.8 fusion.42
  67.0 26.0 %all-reduce.6.cloned.1.call-done = f32[512,256]{1,0:T(8,128)} async-done(((f32[512,256]{1,0:T(8,128)}), f32[512,256]{1,0:T(8,128)}) %all-reduce.6.cloned.1.call-update) | async-done | bytes 524304 | tf_op jit(solution)/shard_map/psum | solution.py:35
  93.1 2.9 fusion.43
  96.3 50.2 %all-gather.6.cloned.1.call-done = f32[4096,256]{1,0:T(8,128)} async-done(((f32[256,256]{1,0:T(8,128)}), f32[4096,256]{1,0:T(8,128)}) %all-gather.6.cloned.1.call-update) | async-done | bytes 4194320 | tf_op jit(solution)/shard_map/all_gather | solution.py:36
  146.5 2.5 reduce_sum.18
  149.2 11.7 %cholesky.172 = f32[128,128]{1,0:T(8,128)S(1)} custom-call(f32[128,128]{1,0:T(8,128)S(1)} %cholesky.270), custom_call_target="Cholesky" | custom-call | tf_op jit(solution)/shard_map/jit(cholesky)/cholesky | solution.py:16
  161.0 9.8 %custom-call.19 = f32[1,128,128]{1,2,0:T(8,128)S(1)} custom-call(f32[1,128,128]{2,1,0:T(8,128)S(1)} %get-tuple-element.73), custom_call_target="InvertDiagBlocksLowerTriangular" | custom-call | tf_op jit(solution)/shard_map/jit(cholesky)/cholesky | solution.py:16
  171.2 11.7 %cholesky.189 = f32[128,128]{1,0:T(8,128)S(1)} custom-call(f32[128,128]{1,0:T(8,128)S(1)} %convolution_subtract_fusion.5), custom_call_target="Cholesky" | custom-call | tf_op jit(solution)/shard_map/jit(cholesky)/cholesky | solution.py:16
  185.2 4.6 while.6
  186.3 1.4 bitcast_dynamic-update-slice_fusion.7
  188.4 1.4 bitcast_dynamic-update-slice_fusion.7
  189.8 19.7 %custom-call.20 = f32[2,128,128]{1,2,0:T(8,128)S(1)} custom-call(f32[2,128,128]{2,1,0:T(8,128)S(1)} %get-tuple-element.26), custom_call_target="InvertDiagBlocksLowerTriangular" | custom-call | tf_op jit(solution)/shard_map/jit(_solve_triangular)/triangular_solve | solution.py:20
  209.5 1.4 fusion.9
  210.9 1.5 convolution_subtract_fusion.2
  212.9 16.1 %fusion.6 = f32[16384,256]{1,0:T(8,128)} fusion(bf16[512,16384]{1,0:T(8,128)(2,1)} %copy-done.2, bf16[128,512]{1,0:T(8,128)(2,1)S(1)} %fusion.23, f32[128,512]{1,0:T(8,128)S(1)} %fusion.9), kind=kOutput, calls=%fused_computation.25 | convolution fusion | flops 4295491584 | bytes 33947648 | tf_op jit(solution)/shard_map/dot_general | solution.py:44
  229.0 296.6 %all-reduce.8.cloned.1.call-done = f32[16384,256]{1,0:T(8,128)} async-done(((f32[16384,256]{1,0:T(8,128)}), f32[16384,256]{1,0:T(8,128)}) %all-reduce.8.cloned.1.call-update) | async-done | bytes 16777232 | tf_op jit(solution)/shard_map/psum | solution.py:47
  525.6 37.8 %fusion.44 = f32[256,256]{0,1:T(8,128)} fusion(f32[16384,256]{1,0:T(8,128)} %all-reduce.8.cloned.1.call-done), kind=kOutput, calls=%fused_computation.95 | convolution fusion | flops 12884901888 | bytes 17039360 | tf_op jit(solution)/shard_map/dot_general | solution.py:24
  563.5 23.0 %all-reduce.10.cloned.1.call-done = f32[256,256]{0,1:T(8,128)} async-done(((f32[256,256]{0,1:T(8,128)}), f32[256,256]{0,1:T(8,128)}) %all-reduce.10.cloned.1.call-update) | async-done | bytes 262160 | tf_op jit(solution)/shard_map/psum | solution.py:48
  586.5 1.1 copy.15
  588.6 11.7 %cholesky.206 = f32[128,128]{1,0:T(8,128)S(1)} custom-call(f32[128,128]{1,0:T(8,128)S(1)} %cholesky.273), custom_call_target="Cholesky" | custom-call | tf_op jit(solution)/shard_map/jit(cholesky)/cholesky | solution.py:16
  600.4 9.8 %custom-call.21 = f32[1,128,128]{1,2,0:T(8,128)S(1)} custom-call(f32[1,128,128]{2,1,0:T(8,128)S(1)} %get-tuple-element.69), custom_call_target="InvertDiagBlocksLowerTriangular" | custom-call | tf_op jit(solution)/shard_map/jit(cholesky)/cholesky | solution.py:16
  610.7 11.7 %cholesky.223 = f32[128,128]{1,0:T(8,128)S(1)} custom-call(f32[128,128]{1,0:T(8,128)S(1)} %convolution_subtract_fusion.4), custom_call_target="Cholesky" | custom-call | tf_op jit(solution)/shard_map/jit(cholesky)/cholesky | solution.py:16
  625.0 3.8 while.5
  625.6 1.3 bitcast_dynamic-update-slice_fusion.6
  627.5 1.3 bitcast_dynamic-update-slice_fusion.6
  628.8 19.7 %custom-call.15 = f32[2,128,128]{1,2,0:T(8,128)S(1)} custom-call(f32[2,128,128]{2,1,0:T(8,128)S(1)} %get-tuple-element.19), custom_call_target="InvertDiagBlocksLowerTriangular" | custom-call | tf_op jit(solution)/shard_map/jit(_solve_triangular)/triangular_solve | solution.py:20
  648.5 10.8 %fusion.3 = f32[128,16384]{1,0:T(8,128)S(1)} fusion(f32[256,16384]{0,1:T(8,128)} %bitcast.115, f32[2,128,128]{1,2,0:T(8,128)S(1)} %custom-call.15), kind=kOutput, calls=%fused_computation.12 | convolution fusion | flops 3221225472 | bytes 16842752 | tf_op jit(solution)/shard_map/jit(_solve_triangular)/triangular_solve | solution.py:20
  659.3 13.4 %convolution_subtract_fusion = f32[128,16384]{0,1:T(8,128)S(1)} fusion(f32[128,16384]{1,0:T(8,128)S(1)} %fusion.3, f32[256,16384]{0,1:T(8,128)S(1)} %bitcast.116, f32[256,256]{1,0:T(8,128)S(1)} %get-tuple-element.227), kind=kOutput, calls=%fused_computation.7 | convolution fusion | flops 3223322624 | bytes 25231360 | tf_op jit(solution)/shard_map/jit(_solve_triangular)/triangular_solve | solution.py:20
  672.7 9.8 %fusion.19 = f32[128,16384]{1,0:T(8,128)} fusion(f32[128,16384]{0,1:T(8,128)S(1)} %convolution_subtract_fusion, f32[2,128,128]{1,2,0:T(8,128)S(1)} %custom-call.15), kind=kOutput, calls=%fused_computation.45 | convolution fusion | flops 3221225472 | bytes 16842752 | tf_op jit(solution)/shard_map/jit(_solve_triangular)/triangular_solve | solution.py:20
  682.5 13.7 %fusion.1 = f32[512,256]{1,0:T(8,128)} fusion(bf16[512,16384]{1,0:T(8,128)(2,1)} %copy-done.2, f32[128,16384]{1,0:T(8,128)} %fusion.19, f32[128,16384]{1,0:T(8,128)} %copy-done.1), kind=kOutput, calls=%fused_computation.11 | convolution fusion | flops 4311744512 | bytes 34078720 | tf_op jit(solution)/shard_map/dot_general | solution.py:35
  696.3 28.8 %all-reduce.12.cloned.1.call-done = f32[512,256]{1,0:T(8,128)} async-done(((f32[512,256]{1,0:T(8,128)}), f32[512,256]{1,0:T(8,128)}) %all-reduce.12.cloned.1.call-update) | async-done | bytes 524304 | tf_op jit(solution)/shard_map/psum | solution.py:35
  725.1 3.0 fusion.45
  728.1 12.4 %multiply_bitcast_fusion = f32[16384,256]{0,1:T(8,128)} fusion(f32[128,16384]{1,0:T(8,128)} %fusion.19, f32[128,16384]{1,0:T(8,128)} %copy-done.1), kind=kLoop, calls=%fused_computation.9 | loop fusion | flops 8388608 | bytes 33554432 | tf_op jit(solution)/shard_map/mul | solution.py:55
  740.5 17.6 %copy.18 = f32[16384,256]{1,0:T(8,128)} copy(f32[16384,256]{0,1:T(8,128)} %multiply_bitcast_fusion) | data formatting | bytes 33554432
  758.0 20.6 %all-gather.8.cloned.1.call-done = f32[4096,256]{1,0:T(8,128)} async-done(((f32[256,256]{1,0:T(8,128)}), f32[4096,256]{1,0:T(8,128)}) %all-gather.8.cloned.1.call-update) | async-done | bytes 4194320 | tf_op jit(solution)/shard_map/all_gather | solution.py:36
  778.7 2.5 reduce_sum.19
  781.3 11.7 %cholesky.240 = f32[128,128]{1,0:T(8,128)S(1)} custom-call(f32[128,128]{1,0:T(8,128)S(1)} %cholesky.276), custom_call_target="Cholesky" | custom-call | tf_op jit(solution)/shard_map/jit(cholesky)/cholesky | solution.py:16
  793.1 9.8 %custom-call.22 = f32[1,128,128]{1,2,0:T(8,128)S(1)} custom-call(f32[1,128,128]{2,1,0:T(8,128)S(1)} %get-tuple-element.65), custom_call_target="InvertDiagBlocksLowerTriangular" | custom-call | tf_op jit(solution)/shard_map/jit(cholesky)/cholesky | solution.py:16
  803.4 11.7 %cholesky.257 = f32[128,128]{1,0:T(8,128)S(1)} custom-call(f32[128,128]{1,0:T(8,128)S(1)} %convolution_subtract_fusion.3), custom_call_target="Cholesky" | custom-call | tf_op jit(solution)/shard_map/jit(cholesky)/cholesky | solution.py:16
  817.9 4.1 while.7
  818.5 1.4 bitcast_dynamic-update-slice_fusion.8
  820.6 1.4 bitcast_dynamic-update-slice_fusion.8
  822.0 19.8 %custom-call.23 = f32[2,128,128]{1,2,0:T(8,128)S(1)} custom-call(f32[2,128,128]{2,1,0:T(8,128)S(1)} %get-tuple-element.27), custom_call_target="InvertDiagBlocksLowerTriangular" | custom-call | tf_op jit(solution)/shard_map/jit(_solve_triangular)/triangular_solve | solution.py:20
  843.4 1.0 copy.17
  (74 shorter events, 12.7 us)
Async XLA Ops:
  7.2 85.9 %all-reduce.6.cloned.1.call-start = ((), (), s32[]{:S(2)}) async-start(), calls=%async_computation | async-start | bytes 1048576 | tf_op jit(solution)/shard_map/psum | solution.py:35
  53.0 6.2 copy-start.2
  67.0 79.5 %all-gather.6.cloned.1.call-start = ((), (), s32[]{:S(2)}) async-start(), calls=%async_computation.4 | async-start | bytes 4456448 | tf_op jit(solution)/shard_map/all_gather | solution.py:36
  96.0 429.6 %all-reduce.8.cloned.1.call-start = ((), (), s32[]{:S(2)}) async-start(), calls=%async_computation.1 | async-start | bytes 33554432 | tf_op jit(solution)/shard_map/psum | solution.py:47
  229.0 357.6 %all-reduce.10.cloned.1.call-start = ((), (), s32[]{:S(2)}) async-start(), calls=%async_computation.2 | async-start | bytes 524288 | tf_op jit(solution)/shard_map/psum | solution.py:48
  563.5 161.6 %all-reduce.12.cloned.1.call-start = ((), (), s32[]{:S(2)}) async-start(), calls=%async_computation.3 | async-start | bytes 1048576 | tf_op jit(solution)/shard_map/psum | solution.py:35
  648.5 10.8 %copy-start = (f32[16384,256]{1,0:T(8,128)S(1)}, f32[16384,256]{1,0:T(8,128)}, u32[]{:S(2)}) copy-start(f32[16384,256]{1,0:T(8,128)} %all-reduce.8.cloned.1.call-done) | copy-start | bytes 50331652
  659.3 13.4 %copy-start.1 = (f32[128,16384]{1,0:T(8,128)}, f32[128,16384]{1,0:T(8,128)S(1)}, u32[]{:S(2)}) copy-start(f32[128,16384]{1,0:T(8,128)S(1)} %fusion.3) | copy-start | bytes 25165828
  696.3 82.4 %all-gather.8.cloned.1.call-start = ((), (), s32[]{:S(2)}) async-start(), calls=%async_computation.5 | async-start | bytes 4456448 | tf_op jit(solution)/shard_map/all_gather | solution.py:36
  740.5 101.4 %copy-start.3 = (f32[512,256]{1,0:T(8,128)S(1)}, f32[512,256]{1,0:T(8,128)}, u32[]{:S(2)}) copy-start(f32[512,256]{1,0:T(8,128)} %all-reduce.12.cloned.1.call-done) | copy-start | bytes 1572868
Sparse Core Ops, SparseCore 0:
  67.1 25.9 all-reduce.5
  96.1 50.3 all-gather.5
  229.1 296.4 all-reduce.7
  563.6 22.9 all-reduce.9
  696.4 28.6 all-reduce.11
  728.2 50.3 all-gather.7
